TPU v7x, 512 devices: a whole 4x8x8 slice. The times are simulated.
512 devices in a mesh: dp: 32 (over z, x), seq: 16 (over y, core).
Axes of the slice: x: 4, y: 8, z: 8, core: 2. Of those that a mesh axis runs over, the one named last changes fastest.
Arguments:
- tokens: bfloat16 [32, 8192, 2048], P('dp', 'seq'), may hold values from -60 to 60
- in_gain: float32 [2048], replicated, may hold values from 0.1 to 1.9
- in_weight: bfloat16 [2048, 2304], P('dp'), may hold values from -0.125 to 0.125
- conv_weight: float32 [4, 2304], replicated, may hold values from -5 to 5
- conv_bias: float32 [2304], replicated, may hold values from -3 to 3
- log_decay: float32 [32, 32, 8192], P('dp', None, 'seq'), may hold values from -0.9 to 0
- skip: float32 [32], replicated, may hold values from 0.05 to 1
- out_gain: float32 [2048], replicated, may hold values from 0.1 to 1.9
- scan_order: int32 [512], replicated, may hold values from 0 to 511, each once
Outputs:
- regrouped: bfloat16 [32, 8192, 2048], P('dp', 'seq')
Inputs may be any that keep to these rules, and one draw needn't show every extreme that they name: Each of the 512 positions appears once; the q-th position of a frame in the next layer's scan is scan_order[q].
All inputs are finite; a program needn't handle non-finite values.
Results may differ from a plain program's by a relative error of at most 0.008.
Values may be sent and summed in bfloat16 or wider, within the bound.
No kernel may reach another device: no remote copies, remote signals or barrier semaphores. Data moves between devices by JAX's collectives and lax.ppermute only.
A program may use at most 128 MiB of HBM per device.

v0:
```python
import jax
import jax.numpy as jnp
from jax import lax
from jax.sharding import PartitionSpec as P

HALF_HEADS = 32
HEADDIM = 64
STATE = 128
GROUP = 128
POSITIONS = 512


def passed_along(block, axis, distance):
    devices = range(lax.axis_size(axis))
    route = [(i - distance, i) for i in devices if i - distance in devices]
    return lax.ppermute(block, axis, route)


def entering_2(part, axis, combine, identity):
    place = lax.axis_index(axis)
    gathered = jax.tree.map(lambda a: lax.all_gather(a, axis), part)
    state = jax.tree.map(lambda a, e: jnp.zeros_like(a) + jnp.asarray(e, a.dtype), part, identity)

    def one(step, state):
        return combine(
            state, jax.tree.map(lambda a: lax.dynamic_index_in_dim(a, step, 0, False), gathered)
        )

    return lax.fori_loop(0, place, one, state)


def project(operand, in_weight):
    whole_weight = lax.all_gather(in_weight, "dp", axis=0, tiled=True)
    return jnp.dot(operand, whole_weight, preferred_element_type=jnp.float32).astype(jnp.bfloat16)


def combine_states(earlier, later):
    return (earlier[0] * later[0], later[0][:, None, None] * earlier[1] + later[1])


def on_device(
    tokens, in_gain, in_weight, conv_weight, conv_bias, log_decay, skip, out_gain, scan_order
):
    own_tokens = tokens[0]
    token_count = own_tokens.shape[0]
    tap_count = conv_weight.shape[0]
    margin = tap_count - 1
    widened = own_tokens.astype(jnp.float32)
    inverse = lax.rsqrt(jnp.mean(widened * widened, axis=1, keepdims=True) + 1e-05)
    normed = (widened * inverse * in_gain[None, :]).astype(jnp.bfloat16)
    projected = project(normed, in_weight)
    earlier_rows = passed_along(projected[token_count - margin :], "seq", 1)
    extended = jnp.concatenate([earlier_rows, projected], axis=0)
    mixed_pre = conv_bias[None, :] + conv_weight[0][None, :] * extended[0:token_count].astype(
        jnp.float32
    )
    for offset in range(1, tap_count):
        mixed_pre = mixed_pre + conv_weight[offset][None, :] * extended[
            offset : offset + token_count
        ].astype(jnp.float32)
    mixed = jax.nn.silu(mixed_pre).astype(jnp.bfloat16)
    inner_width = HALF_HEADS * HEADDIM
    x_heads = mixed[:, :inner_width].reshape(token_count, HALF_HEADS, HEADDIM)
    b_vectors = mixed[:, inner_width : inner_width + STATE]
    c_vectors = mixed[:, inner_width + STATE :]
    own_decay = log_decay[0]
    block_count = token_count // GROUP
    places = jnp.arange(GROUP)
    causal = places[None, :] <= places[:, None]
    intra_parts = []
    block_states = []
    closings = []
    cumulatives = []
    device_state = jnp.zeros((HALF_HEADS, HEADDIM, STATE), jnp.float32)
    device_decay = jnp.ones((HALF_HEADS,), jnp.float32)
    for block_index in range(block_count):
        first_row = block_index * GROUP
        end_row = first_row + GROUP
        x_block = x_heads[first_row:end_row]
        b_block = b_vectors[first_row:end_row]
        c_block = c_vectors[first_row:end_row]
        decay_block = own_decay[:, first_row:end_row]
        cumulative = jnp.cumsum(decay_block, axis=1)
        step_size = -decay_block
        scores = lax.dot_general(
            c_block, b_block, (((1,), (1,)), ((), ())), preferred_element_type=jnp.float32
        )
        log_gap = cumulative[:, :, None] - cumulative[:, None, :]
        decay_mask = jnp.exp(jnp.where(causal[None], log_gap, -1e30))
        weights = (scores[None] * decay_mask * step_size[:, None, :]).astype(jnp.bfloat16)
        intra_parts.append(
            jnp.einsum("hts,shp->thp", weights, x_block, preferred_element_type=jnp.float32)
        )
        closing = cumulative[:, -1:]
        scaled = (
            (jnp.exp(closing - cumulative) * step_size).T[:, :, None] * x_block.astype(jnp.float32)
        ).astype(jnp.bfloat16)
        block_state = jnp.einsum("shp,sn->hpn", scaled, b_block, preferred_element_type=jnp.float32)
        fading = jnp.exp(closing[:, 0])
        device_state = fading[:, None, None] * device_state + block_state
        device_decay = device_decay * fading
        block_states.append(block_state)
        closings.append(fading)
        cumulatives.append(cumulative)
    carried = entering_2(
        (device_decay, device_state),
        "seq",
        combine_states,
        (jnp.ones_like(device_decay), jnp.zeros_like(device_state)),
    )
    entering = carried[1]
    outputs = []
    for block_index in range(block_count):
        first_row = block_index * GROUP
        c_block = c_vectors[first_row : first_row + GROUP]
        inter = jnp.einsum(
            "tn,hpn->thp",
            c_block,
            entering.astype(jnp.bfloat16),
            preferred_element_type=jnp.float32,
        )
        inter = inter * jnp.exp(cumulatives[block_index]).T[:, :, None]
        outputs.append(intra_parts[block_index] + inter)
        entering = closings[block_index][:, None, None] * entering + block_states[block_index]
    ssm_out = jnp.concatenate(outputs, axis=0) + skip[None, :, None] * x_heads.astype(jnp.float32)
    head_scale = lax.rsqrt(jnp.mean(ssm_out * ssm_out, axis=2, keepdims=True) + 1e-05)
    normalized = (ssm_out * head_scale * out_gain.reshape(HALF_HEADS, HEADDIM)[None]).astype(
        jnp.bfloat16
    )
    frames_here = token_count // POSITIONS
    framed = normalized.reshape(frames_here, POSITIONS, inner_width)
    picked = jnp.take(framed, scan_order, axis=1).transpose(1, 0, 2)
    seq_count = lax.axis_size("seq")
    outgoing = picked.reshape(seq_count, POSITIONS // seq_count, frames_here, inner_width)
    arrived = lax.all_to_all(outgoing, "seq", split_axis=0, concat_axis=2, tiled=True)
    return arrived.reshape(1, token_count, inner_width)


def solution(mesh):
    in_specs = (
        P("dp", "seq", None),
        P(),
        P("dp", None),
        P(),
        P(),
        P("dp", None, "seq"),
        P(),
        P(),
        P(),
    )
    out_specs = P("dp", "seq", None)
    return jax.shard_map(
        on_device, mesh=mesh, in_specs=in_specs, out_specs=out_specs, check_vma=False
    )
```

profile of v0, /device:TPU:1, one launch (start us, length us, event | category | flops | bytes accessed | tf_op | source)
XLA Modules:
  0.0 378.1 jit_solution(2298110102641624891)
XLA Ops:
  10.5 2.1 fusion
  13.3 111.3 %all-gather.5.cloned.1.call-done = bf16[2048,2304]{1,0:T(8,128)(2,1)} async-done(((bf16[64,2304]{1,0:T(8,128)(2,1)}), bf16[2048,2304]{1,0:T(8,128)(2,1)}) %all-gather.5.cloned.1.call-update) | async-done | bytes 9437200 | tf_op jit(solution)/shard_map/all_gather | solution.py:33
  124.6 9.1 %convolution_convert_fusion = bf16[512,2304]{1,0:T(8,128)(2,1)S(1)} fusion(bf16[2048,2304]{1,0:T(8,128)(2,1)} %all-gather.5.cloned.1.call-done, bf16[1,512,2048]{2,1,0:T(8,128)(2,1)S(1)} %copy-done.15, f32[2048]{0:T(1024)S(1)} %copy-done.41, f32[512]{0:T(512)S(1)} %add_rsqrt_fusion.1), kind=kOutput, calls=%fused_computation.6 | convolution fusion | flops 4837212160 | bytes 13903872 | tf_op jit(solution)/shard_map/dot_general | solution.py:34
  133.8 4.4 %collective-permute-start = (bf16[3,2304]{1,0:T(4,128)(2,1)S(1)}, bf16[3,2304]{1,0:T(4,128)(2,1)S(1)}, u32[]{:S(2)}, u32[]{:S(2)}) collective-permute-start(bf16[3,2304]{1,0:T(4,128)(2,1)S(1)} %slice.152), channel_id=1, source_target_pairs={{0,1},{1,2},{2,3},{3,4},{4,5},{5,6},{6,7},{7,8},{8,9},{9,10},{10,1... | collective-permute-start | bytes 41480 | tf_op jit(solution)/shard_map/ppermute | solution.py:16
  140.0 3.4 multiply_convert_fusion
  143.4 1.5 fusion.85
  144.9 2.0 copy.46
  148.2 1.3 copy.49
  149.6 1.3 fusion.42
  150.9 1.7 fusion.43
  154.1 1.4 convolution_add_fusion
  158.2 24.8 %all-reduce = f32[512]{0:T(512)S(1)} all-reduce(f32[512]{0:T(512)S(1)} %dynamic-update-slice), channel_id=2, replica_groups=mesh['dp'=32,'seq'=16] {'seq'}, use_global_device_ids=true, to_apply=%add | all-reduce | flops 512 | bytes 4096
  188.3 2.5 slice_convert_fusion
  190.8 5.4 %copy.54 = f32[512,2048]{0,1:T(8,128)} copy(f32[512,2048]{1,0:T(8,128)} %slice_convert_fusion) | data formatting | bytes 8388608 | tf_op jit(solution)/shard_map/convert_element_type | solution.py:125
  196.8 3.0 convolution_bitcast_fusion.3
  199.8 1.9 convolution_bitcast_fusion.2
  201.7 1.9 convolution_bitcast_fusion.1
  203.6 1.9 convolution_bitcast_fusion
  205.5 45.8 %all-gather.7.cloned.1.call-done = f32[512,64,128]{2,1,0:T(8,128)} async-done(((f32[32,64,128]{2,1,0:T(8,128)}), f32[512,64,128]{2,1,0:T(8,128)}) %all-gather.7.cloned.1.call-update) | async-done | bytes 16777232 | tf_op jit(solution)/shard_map/all_gather | solution.py:21
  251.4 2.3 while.12
  252.1 1.4 bitcast_add_fusion.2
  253.8 1.9 multiply_add_fusion
  262.2 2.5 mul.426
  264.7 5.5 %copy.55 = f32[512,2048]{1,0:T(8,128)} copy(f32[512,2048]{0,1:T(8,128)} %bitcast.90) | data formatting | bytes 8388608 | tf_op jit(solution)/shard_map/mul | solution.py:127
  270.2 1.3 copy.50
  271.6 1.3 copy.51
  274.2 1.3 copy.53
  275.6 4.3 %fusion.5 = bf16[512,2048]{1,0:T(8,128)(2,1)S(1)} fusion(f32[512,2048]{1,0:T(8,128)} %copy.55, f32[128,2048]{1,0:T(8,128)} %copy.53, f32[128,2048]{1,0:T(8,128)} %copy.52, f32[128,2048]{1,0:T(8,128)} %copy.51, f32[128,2048]{1,0:T(8,128)S(1)} %copy-done.13, f32[2048]{0:T(1024)S(1)} %copy-done.31, f32[2048]{0:T(1024)S(1)} %copy-done.23, ...), kind=kLoop, calls=%fused_computation.13 | loop fusion | flops 9437184 | bytes 12599296 | tf_op jit(solution)/shard_map/convert_element_type | solution.py:127
  279.9 3.3 gather_fusion
  283.2 1.8 broadcast_select_fusion
  285.1 83.7 %all_to_all.15 = bf16[16,32,1,2048]{3,1,2,0:T(8,128)(2,1)S(1)} all-to-all(bf16[16,32,1,2048]{3,1,2,0:T(8,128)(2,1)S(1)} %broadcast_select_fusion), channel_id=1, replica_groups=mesh['dp'=32,'seq'=16] {'seq'}, dimensions={0} | all-to-all | bytes 4194304 | tf_op jit(solution)/shard_map/all_to_all | solution.py:135
  368.8 2.5 copy.57
  (130 shorter events, 25.6 us)
Async XLA Ops:
  6.5 6.1 %copy-start.20 = (f32[1,32,512]{2,1,0:T(8,128)S(1)}, f32[1,32,512]{2,1,0:T(8,128)}, u32[]{:S(2)}) copy-start(f32[1,32,512]{2,1,0:T(8,128)} %param.16) | copy-start | bytes 196612
  6.5 118.1 %copy-start.15 = (bf16[1,512,2048]{2,1,0:T(8,128)(2,1)S(1)}, bf16[1,512,2048]{2,1,0:T(8,128)(2,1)}, u32[]{:S(2)}) copy-start(bf16[1,512,2048]{2,1,0:T(8,128)(2,1)} %param.11) | copy-start | bytes 6291460
  6.5 118.1 %copy-start.41 = (f32[2048]{0:T(1024)S(1)}, f32[2048]{0:T(1024)}, u32[]{:S(2)}) copy-start(f32[2048]{0:T(1024)} %param.12) | copy-start | bytes 24580
  6.5 118.1 %all-gather.5.cloned.1.call-start = ((), (), s32[]{:S(2)}) async-start(), calls=%async_computation.1 | async-start | bytes 9732096 | tf_op jit(solution)/shard_map/all_gather | solution.py:33
  7.3 244.0 %all-gather.7.cloned.1.call-start = ((), (), s32[]{:S(2)}) async-start(), calls=%async_computation.2 | async-start | bytes 17825792 | tf_op jit(solution)/shard_map/all_gather | solution.py:21
  13.3 124.8 %copy-start.22 = (f32[4,2304]{1,0:T(4,128)S(1)}, f32[4,2304]{1,0:T(4,128)}, u32[]{:S(2)}) copy-start(f32[4,2304]{1,0:T(4,128)} %param.14) | copy-start | bytes 110596
  13.3 126.7 %copy-start.29 = (f32[2304]{0:T(1024)S(1)}, f32[2304]{0:T(1024)}, u32[]{:S(2)}) copy-start(f32[2304]{0:T(1024)} %param.15) | copy-start | bytes 27652
  133.8 6.2 %collective-permute-start = (bf16[3,2304]{1,0:T(4,128)(2,1)S(1)}, bf16[3,2304]{1,0:T(4,128)(2,1)S(1)}, u32[]{:S(2)}, u32[]{:S(2)}) collective-permute-start(bf16[3,2304]{1,0:T(4,128)(2,1)S(1)} %slice.152), channel_id=1, source_target_pairs={{0,1},{1,2},{2,3},{3,4},{4,5},{5,6},{6,7},{7,8},{8,9},{9,10},{10,1... | collective-permute-start | bytes 41480 | tf_op jit(solution)/shard_map/ppermute | solution.py:16
  143.3 115.0 %copy-start = (bf16[512,2304]{1,0:T(8,128)(2,1)}, bf16[512,2304]{1,0:T(8,128)(2,1)S(1)}, u32[]{:S(2)}) copy-start(bf16[512,2304]{1,0:T(8,128)(2,1)S(1)} %multiply_convert_fusion) | copy-start | bytes 7077892
  149.5 3.1 copy-start.21
  149.5 4.5 %copy-start.34 = (f32[32]{0:T(128)S(1)}, f32[32]{0:T(128)}, u32[]{:S(2)}) copy-start(f32[32]{0:T(128)} %exp.131) | copy-start | bytes 388
  149.5 4.5 %copy-start.36 = (f32[32]{0:T(128)S(1)}, f32[32]{0:T(128)}, u32[]{:S(2)}) copy-start(f32[32]{0:T(128)} %exp.132) | copy-start | bytes 388
  149.6 4.5 %copy-start.39 = (f32[32]{0:T(128)S(1)}, f32[32]{0:T(128)}, u32[]{:S(2)}) copy-start(f32[32]{0:T(128)} %get-tuple-element.90) | copy-start | bytes 388
  149.6 4.5 %copy-start.40 = (f32[32]{0:T(128)S(1)}, f32[32]{0:T(128)}, u32[]{:S(2)}) copy-start(f32[32]{0:T(128)} %exp.130) | copy-start | bytes 388
  150.9 2.1 copy-start.1
  190.8 6.0 %copy-start.27 = (f32[32,128]{1,0:T(8,128)S(1)}, f32[32,128]{1,0:T(8,128)}, u32[]{:S(2)}) copy-start(f32[32,128]{1,0:T(8,128)} %get-tuple-element.73) | copy-start | bytes 49156
  196.2 3.6 copy-start.14
  196.2 3.6 copy-start.26
  196.2 3.6 copy-start.28
  251.4 2.4 copy-start.33
  251.4 2.4 copy-start.37
  256.0 4.3 %copy-start.4 = (f32[128,32,64]{0,2,1:T(8,128)}, f32[128,32,64]{0,2,1:T(8,128)S(1)}, u32[]{:S(2)}) copy-start(f32[128,32,64]{0,2,1:T(8,128)S(1)} %fusion.17) | copy-start | bytes 3145732
  256.0 2.0 copy-start.19
  258.0 2.3 copy-start.6
  258.3 2.9 copy-start.3
  258.3 2.8 copy-start.38
  264.7 5.5 %copy-start.5 = (f32[128,32,64]{0,2,1:T(8,128)S(1)}, f32[128,32,64]{0,2,1:T(8,128)}, u32[]{:S(2)}) copy-start(f32[128,32,64]{0,2,1:T(8,128)} %copy-done.4) | copy-start | bytes 3145732
  271.6 2.7 copy-start.9
  272.9 2.6 copy-start.23
  272.9 2.6 copy-start.31
  275.6 4.3 %copy-start.30 = (s32[1024]{0:T(1024)S(1)}, s32[1024]{0:T(1024)}, u32[]{:S(2)}) copy-start(s32[1024]{0:T(1024)} %pad_clamp_fusion) | copy-start | bytes 12292
  279.9 3.3 copy-start.32
  (13 other events, 20.1 us)
Sparse Core Ops, SparseCore 0:
  10.5 114.0 all-gather.4
  155.6 95.6 all-gather.6
where the time goes:
time: 380 us; the launch traced here: 378 us
  waiting for transfers between devices  158 us (42%)
  blocking collectives  108 us (28%)
  local copies, waits for them, and re-layouts  44 us (12%)
  matrix products  24.4 us (6%)
  other arithmetic  24.2 us (6%)
  between operations  14.5 us (4%)
  starting transfers between devices  4.43 us (1%)
    all_gather x1, waiting for transfers between devices, project(): whole_weight = lax.all_gather(in_weight, 'dp', axis=0, tiled=True)  111 us
    all_to_all x1, blocking collectives, on_device(): lax.all_to_all(outgoing, 'seq', split_axis=0, concat_axis=2, tiled=True)  83.7 us
    all_gather x1, waiting for transfers between devices, entering_2(): gathered = jax.tree.map(lambda a: lax.all_gather(a, axis), part)  45.8 us
    unnamed x1, blocking collectives  24.8 us
    dot_general x1, matrix products, project(): jnp.dot(operand, whole_weight, preferred_element_type=jnp.float32)  9.08 us
    dot_general x4, matrix products, on_device(): jnp.einsum('hts,shp->thp', weights, x_block, preferred_element_type=jnp.f...  8.69 us
    mul x2, local copies, waits for them, and re-layouts, on_device(): ssm_out * head_scale * out_gain.reshape(HALF_HEADS, HEADDIM)[None]  8.02 us
  transfers between devices with their start and end apart: 3, of which 2 were waited for; matrix products, arithmetic and copies ran while one was open for 9% of the time, Pallas kernels for 0%

commit v1 on v0

--- a/solution.py
+++ b/solution.py
@@ -30,7 +30,9 @@
 
 
 def project(operand, in_weight):
-    whole_weight = lax.all_gather(in_weight, "dp", axis=0, tiled=True)
+    whole_weight = jnp.concatenate(
+        lax.all_to_all(jnp.stack([in_weight] * lax.axis_size("dp")), "dp", 0, 0), axis=0
+    )
     return jnp.dot(operand, whole_weight, preferred_element_type=jnp.float32).astype(jnp.bfloat16)
 
 

time: 380 us -> 506 us (1.33)
  waiting for transfers between devices: 158 us -> 268 us
  starting transfers between devices: 4.43 us -> 18.8 us
    all_to_all x0 -> x1, waiting for transfers between devices: none -> 207 us  [project(): lax.all_to_all(jnp.stack([in_weight] * lax.axis_size('dp')), 'dp', 0, 0)]
    all_gather x1 -> x0, waiting for transfers between devices: 111 us -> none  [project(): whole_weight = lax.all_gather(in_weight, 'dp', axis=0, tiled=True)]
    all_gather x1, waiting for transfers between devices: 45.8 us -> 60.5 us  [entering_2(): gathered = jax.tree.map(lambda a: lax.all_gather(a, axis), part)]
    all_to_all x0 -> x1, starting transfers between devices: none -> 13.9 us  [project(): lax.all_to_all(jnp.stack([in_weight] * lax.axis_size('dp')), 'dp', 0, 0)]
    another operation x1 -> x2, local copies, waits for them, and re-layouts: 0.11 us -> 5.78 us  [the longest x1 5.68 us: project(): jnp.stack([in_weight] * lax.axis_size('dp'))]
  transfers between devices with their start and end apart: 3 -> 3, of which waited for: 2 -> 2; matrix products, arithmetic and copies ran while one was open for 9% -> 6% of each run, Pallas kernels for 0% -> 0%
where the time goes in v1:
time: 506 us; the launch traced here: 505 us
  waiting for transfers between devices  268 us (53%)
  blocking collectives  108 us (21%)
  local copies, waits for them, and re-layouts  48.9 us (10%)
  matrix products  24.4 us (5%)
  other arithmetic  22.6 us (4%)
  starting transfers between devices  18.8 us (4%)
  between operations  14.5 us (3%)
    all_to_all x1, waiting for transfers between devices, project(): lax.all_to_all(jnp.stack([in_weight] * lax.axis_size('dp')), 'dp', 0, 0)  207 us
    all_to_all x1, blocking collectives, on_device(): lax.all_to_all(outgoing, 'seq', split_axis=0, concat_axis=2, tiled=True)  83.9 us
    all_gather x1, waiting for transfers between devices, entering_2(): gathered = jax.tree.map(lambda a: lax.all_gather(a, axis), part)  60.5 us
    unnamed x1, blocking collectives  23.8 us
    all_to_all x1, starting transfers between devices, project(): lax.all_to_all(jnp.stack([in_weight] * lax.axis_size('dp')), 'dp', 0, 0)  13.9 us
  transfers between devices with their start and end apart: 3, of which 2 were waited for; matrix products, arithmetic and copies ran while one was open for 6% of the time, Pallas kernels for 0%

profile of v1, /device:TPU:1, one launch (start us, length us, event | category | flops | bytes accessed | tf_op | source)
XLA Modules:
  0.0 504.6 jit_solution(2698913618406828252)
XLA Ops:
  6.5 5.7 %stack.2 = bf16[32,64,2304]{2,1,0:T(8,128)(2,1)} broadcast(bf16[64,2304]{1,0:T(8,128)(2,1)} %param.13), dimensions={1,2} | broadcast | bytes 9732096 | tf_op jit(solution)/shard_map/stack | solution.py:34
  12.2 13.9 %all-to-all-start = ((bf16[32,64,2304]{2,1,0:T(8,128)(2,1)}), bf16[32,64,2304]{2,1,0:T(8,128)(2,1)}, u32[]{:S(2)}, u32[]{:S(2)}) async-start(bf16[32,64,2304]{2,1,0:T(8,128)(2,1)} %stack.2), calls=%async_computation | async-start | bytes 18874368 | tf_op jit(solution)/shard_map/all_to_all | solution.py:34
  29.9 207.0 %all-to-all-done = bf16[32,64,2304]{2,1,0:T(8,128)(2,1)} async-done(((bf16[32,64,2304]{2,1,0:T(8,128)(2,1)}), bf16[32,64,2304]{2,1,0:T(8,128)(2,1)}, u32[]{:S(2)}, u32[]{:S(2)}) %all-to-all-start) | async-done | bytes 9437216 | tf_op jit(solution)/shard_map/all_to_all | solution.py:34
  236.9 9.1 %convolution_convert_fusion = bf16[512,2304]{1,0:T(8,128)(2,1)S(1)} fusion(bf16[2048,2304]{1,0:T(8,128)(2,1)} %bitcast.3, bf16[1,512,2048]{2,1,0:T(8,128)(2,1)S(1)} %copy-done.15, f32[2048]{0:T(1024)S(1)} %copy-done.41, f32[512]{0:T(512)S(1)} %add_rsqrt_fusion.1), kind=kOutput, calls=%fused_computation.6 | convolution fusion | flops 4837212160 | bytes 13903872 | tf_op jit(solution)/shard_map/dot_general | solution.py:36
  246.1 4.8 collective-permute-start
  252.6 3.4 multiply_convert_fusion
  255.9 1.5 fusion.85
  257.5 2.0 copy.46
  260.8 1.3 copy.49
  262.2 1.3 fusion.42
  263.5 1.7 fusion.43
  266.6 1.4 convolution_add_fusion
  270.7 23.8 %all-reduce = f32[512]{0:T(512)S(1)} all-reduce(f32[512]{0:T(512)S(1)} %dynamic-update-slice), channel_id=2, replica_groups=mesh['dp'=32,'seq'=16] {'seq'}, use_global_device_ids=true, to_apply=%add | all-reduce | flops 512 | bytes 4096
  299.8 2.5 slice_convert_fusion
  302.4 5.5 %copy.54 = f32[512,2048]{0,1:T(8,128)} copy(f32[512,2048]{1,0:T(8,128)} %slice_convert_fusion) | data formatting | bytes 8388608 | tf_op jit(solution)/shard_map/convert_element_type | solution.py:127
  308.4 3.0 convolution_bitcast_fusion.3
  311.4 1.9 convolution_bitcast_fusion.2
  313.4 1.9 convolution_bitcast_fusion.1
  315.3 1.9 convolution_bitcast_fusion
  317.2 60.5 %all-gather.4.cloned.1.call-done = f32[512,64,128]{2,1,0:T(8,128)} async-done(((f32[32,64,128]{2,1,0:T(8,128)}), f32[512,64,128]{2,1,0:T(8,128)}) %all-gather.4.cloned.1.call-update) | async-done | bytes 16777232 | tf_op jit(solution)/shard_map/all_gather | solution.py:21
  377.8 2.4 while.12
  378.6 1.4 bitcast_add_fusion.2
  380.2 1.9 multiply_add_fusion
  388.6 2.5 mul.429
  391.2 5.5 %copy.55 = f32[512,2048]{1,0:T(8,128)} copy(f32[512,2048]{0,1:T(8,128)} %bitcast.87) | data formatting | bytes 8388608 | tf_op jit(solution)/shard_map/mul | solution.py:129
  396.6 1.3 copy.50
  398.0 1.3 copy.51
  401.9 4.3 fusion.5
  406.3 3.3 gather_fusion
  409.6 1.8 broadcast_select_fusion
  411.4 83.9 %all_to_all.20 = bf16[16,32,1,2048]{3,1,2,0:T(8,128)(2,1)S(1)} all-to-all(bf16[16,32,1,2048]{3,1,2,0:T(8,128)(2,1)S(1)} %broadcast_select_fusion), channel_id=1, replica_groups=mesh['dp'=32,'seq'=16] {'seq'}, dimensions={0} | all-to-all | bytes 4194304 | tf_op jit(solution)/shard_map/all_to_all | solution.py:137
  495.3 2.5 copy.57
  (130 shorter events, 25.8 us)
Async XLA Ops:
  12.2 14.0 %copy-start.20 = (f32[1,32,512]{2,1,0:T(8,128)S(1)}, f32[1,32,512]{2,1,0:T(8,128)}, u32[]{:S(2)}) copy-start(f32[1,32,512]{2,1,0:T(8,128)} %param.16) | copy-start | bytes 196612
  12.2 16.5 %copy-start.15 = (bf16[1,512,2048]{2,1,0:T(8,128)(2,1)S(1)}, bf16[1,512,2048]{2,1,0:T(8,128)(2,1)}, u32[]{:S(2)}) copy-start(bf16[1,512,2048]{2,1,0:T(8,128)(2,1)} %param.11) | copy-start | bytes 6291460
  12.2 224.7 %all-to-all-start = ((bf16[32,64,2304]{2,1,0:T(8,128)(2,1)}), bf16[32,64,2304]{2,1,0:T(8,128)(2,1)}, u32[]{:S(2)}, u32[]{:S(2)}) async-start(bf16[32,64,2304]{2,1,0:T(8,128)(2,1)} %stack.2), calls=%async_computation | async-start | bytes 18874368 | tf_op jit(solution)/shard_map/all_to_all | solution.py:34
  26.2 210.7 %copy-start.41 = (f32[2048]{0:T(1024)S(1)}, f32[2048]{0:T(1024)}, u32[]{:S(2)}) copy-start(f32[2048]{0:T(1024)} %param.12) | copy-start | bytes 24580
  26.2 351.5 %all-gather.4.cloned.1.call-start = ((), (), s32[]{:S(2)}) async-start(), calls=%async_computation.2 | async-start | bytes 17825792 | tf_op jit(solution)/shard_map/all_gather | solution.py:21
  236.9 14.0 %copy-start.22 = (f32[4,2304]{1,0:T(4,128)S(1)}, f32[4,2304]{1,0:T(4,128)}, u32[]{:S(2)}) copy-start(f32[4,2304]{1,0:T(4,128)} %param.14) | copy-start | bytes 110596
  236.9 15.6 %copy-start.29 = (f32[2304]{0:T(1024)S(1)}, f32[2304]{0:T(1024)}, u32[]{:S(2)}) copy-start(f32[2304]{0:T(1024)} %param.15) | copy-start | bytes 27652
  246.1 6.5 %collective-permute-start = (bf16[3,2304]{1,0:T(4,128)(2,1)S(1)}, bf16[3,2304]{1,0:T(4,128)(2,1)S(1)}, u32[]{:S(2)}, u32[]{:S(2)}) collective-permute-start(bf16[3,2304]{1,0:T(4,128)(2,1)S(1)} %slice.152), channel_id=1, source_target_pairs={{0,1},{1,2},{2,3},{3,4},{4,5},{5,6},{6,7},{7,8},{8,9},{9,10},{10,1... | collective-permute-start | bytes 41480 | tf_op jit(solution)/shard_map/ppermute | solution.py:16
  255.9 128.8 %copy-start = (bf16[512,2304]{1,0:T(8,128)(2,1)}, bf16[512,2304]{1,0:T(8,128)(2,1)S(1)}, u32[]{:S(2)}) copy-start(bf16[512,2304]{1,0:T(8,128)(2,1)S(1)} %multiply_convert_fusion) | copy-start | bytes 7077892
  262.1 3.1 copy-start.21
  262.1 4.5 copy-start.34
  262.1 4.5 copy-start.36
  262.1 4.5 copy-start.39
  262.2 4.5 copy-start.40
  263.5 2.1 copy-start.1
  302.4 6.1 %copy-start.27 = (f32[32,128]{1,0:T(8,128)S(1)}, f32[32,128]{1,0:T(8,128)}, u32[]{:S(2)}) copy-start(f32[32,128]{1,0:T(8,128)} %get-tuple-element.73) | copy-start | bytes 49156
  307.8 3.6 copy-start.14
  307.8 3.6 copy-start.26
  307.8 3.6 copy-start.28
  377.8 2.4 copy-start.33
  377.8 2.4 copy-start.37
  382.4 4.3 copy-start.4
  382.4 2.0 copy-start.19
  384.4 2.3 copy-start.6
  384.7 2.9 copy-start.3
  384.7 2.9 copy-start.38
  391.1 5.5 %copy-start.5 = (f32[128,32,64]{0,2,1:T(8,128)S(1)}, f32[128,32,64]{0,2,1:T(8,128)}, u32[]{:S(2)}) copy-start(f32[128,32,64]{0,2,1:T(8,128)} %copy-done.4) | copy-start | bytes 3145732
  398.0 2.7 copy-start.9
  399.3 2.6 copy-start.23
  399.3 2.6 copy-start.31
  401.9 4.4 copy-start.30
  406.3 3.3 copy-start.32
  (13 other events, 20.1 us)
Sparse Core Ops, SparseCore 0:
  268.1 109.5 all-gather.3
